TPU v7x, 512 devices: a whole 4x4x16 slice. The times are simulated.
512 devices in a mesh: win: 64 (over z, x), rcv: 8 (over y, core).
Axes of the slice: x: 4, y: 4, z: 16, core: 2. Of those that a mesh axis runs over, the one named last changes fastest.
Arguments:
- spectra: bfloat16 [128, 2, 128, 4096], P('win', None, 'rcv'), may hold values from -6 to 6
- source_channel: int32 [8], replicated, may hold values from 0 to 127
Outputs:
- stack: float32 [512, 8, 128], P('win', None, 'rcv')
All inputs are finite; a program needn't handle non-finite values.
Results may differ from a plain program's by a relative error of at most 0.0011.
Values may be sent and summed in bfloat16 or wider, within the bound.
A program may use at most 64 MiB of HBM per device.

v0:
```python
import jax
import jax.numpy as jnp
from jax import lax
from jax.sharding import PartitionSpec as P

L = 512
ITERS = 5


TUKEY = 4.685
EPSILON = 1e-06


def copy_for_each(value, axis):
    length = lax.axis_size(axis)
    return lax.all_to_all(
        jnp.broadcast_to(value[None], (length, *value.shape)), axis, 0, 0, tiled=True
    )


def taken_together(value, axis):
    return copy_for_each(value, axis).astype(jnp.float32).sum(axis=0)


def make_basis(bin_count, lag_count):
    freq = jnp.arange(bin_count, dtype=jnp.int32)
    shifts = jnp.arange(lag_count, dtype=jnp.int32) - lag_count // 2
    phase = shifts[:, None] * freq[None, :] % (2 * bin_count)
    angle = phase.astype(jnp.float32) * (2.0 * jnp.pi / (2 * bin_count))
    factor = jnp.where(freq == 0, 1.0, 2.0).astype(jnp.float32) / jnp.sqrt(
        jnp.float32(8 * bin_count)
    )
    table = jnp.concatenate(
        [jnp.cos(angle) * factor[None, :], -jnp.sin(angle) * factor[None, :]], axis=1
    )
    return table.astype(jnp.bfloat16)


def bisquare_stack(samples):
    center = jnp.mean(samples, axis=0)
    for iteration in range(ITERS):
        deviation = samples - center
        squared = deviation * deviation
        scale_two = jnp.mean(squared, axis=0) + EPSILON
        ratio = squared / (TUKEY * TUKEY * scale_two)
        weight = jnp.where(ratio < 1.0, (1.0 - ratio) * (1.0 - ratio), 0.0)
        center = jnp.sum(weight * samples, axis=0) / jnp.sum(weight, axis=0)
    return center


def per_device(spectra, source_channel):
    win_count = spectra.shape[0]
    chan_count = spectra.shape[2]
    bin_count = spectra.shape[3]
    source_count = source_channel.shape[0]
    channels = lax.axis_index("rcv") * chan_count + lax.iota(jnp.int32, chan_count)
    onehot = (source_channel[:, None] == channels[None, :]).astype(jnp.bfloat16)
    own_part = jnp.einsum("sr,wcrf->wcsf", onehot, spectra, preferred_element_type=jnp.float32)
    picked = (
        taken_together(own_part.astype(jnp.bfloat16), "rcv")
        .astype(jnp.float32)
        .astype(jnp.bfloat16)
    )
    source_float = picked.astype(jnp.float32)
    receiver_float = spectra.astype(jnp.float32)
    real_a = source_float[:, 0][:, :, None, :]
    imag_b = source_float[:, 1][:, :, None, :]
    real_p = receiver_float[:, 0][:, None, :, :]
    imag_q = receiver_float[:, 1][:, None, :, :]
    pair_count = source_count * chan_count
    real_part = (real_a * real_p + imag_b * imag_q).reshape(win_count, pair_count, bin_count)
    imag_part = (imag_b * real_p - real_a * imag_q).reshape(win_count, pair_count, bin_count)
    cross = jnp.concatenate([real_part, imag_part], axis=2).astype(jnp.bfloat16)
    basis = make_basis(bin_count, L)
    corr = jnp.einsum("lk,wpk->wlp", basis, cross, preferred_element_type=jnp.float32)
    block = L // lax.axis_size("win")
    regrouped = lax.all_to_all(corr, "win", split_axis=1, concat_axis=0, tiled=True)
    result = bisquare_stack(regrouped)
    return result.reshape(block, source_count, chan_count)


def solution(mesh):
    return jax.shard_map(
        per_device,
        mesh=mesh,
        in_specs=(P("win", None, "rcv", None), P()),
        out_specs=P("win", None, "rcv"),
        check_vma=False,
    )
```

profile of v0, /device:TPU:1, one launch (start us, length us, event | category | flops | bytes accessed | tf_op | source)
XLA Modules:
  0.0 104.7 jit_solution(7128069527054088099)
XLA Ops:
  0.0 0.0 copy-start.1
  0.0 1.4 %fusion.9 = bf16[2,2,8,4096]{3,2,1,0:T(8,128)(2,1)S(1)} fusion(bf16[2,2,16,4096]{3,2,1,0:T(8,128)(2,1)} %param.2, s32[16]{0:T(128)S(1)} %iota_add_fusion.1, s32[8]{0:T(128)} %param.3), kind=kOutput, calls=%fused_computation.16 | convolution fusion | flops 4325504 | bytes 786528 | tf_op jit(solution)/shard_map/sr,wcrf->wcsf/dot_general | solution.py:58
  1.4 1.6 %broadcast_in_dim.18 = bf16[8,2,2,8,4096]{4,3,2,1,0:T(8,128)(2,1)} broadcast(bf16[2,2,8,4096]{3,2,1,0:T(8,128)(2,1)S(1)} %fusion.9), dimensions={1,2,3,4} | broadcast | bytes 2359296 | tf_op jit(solution)/shard_map/broadcast_in_dim | solution.py:17
  3.0 10.3 %all-to-all-start = ((bf16[8,2,2,8,4096]{4,3,2,1,0:T(8,128)(2,1)}), bf16[8,2,2,8,4096]{4,3,2,1,0:T(8,128)(2,1)S(1)}, u32[]{:S(2)}, u32[]{:S(2)}) async-start(bf16[8,2,2,8,4096]{4,3,2,1,0:T(8,128)(2,1)} %broadcast_in_dim.18), calls=%async_computation | async-start | bytes 4194304 | tf_op jit(solution)/shard_map/all_to_all | solution.py:16
  13.4 0.0 copy-done.1
  13.4 0.1 convert_element_type.25
  13.5 0.1 slice_bitcast_fusion.1
  13.6 36.0 %multiply_convert_fusion.1 = (bf16[512,4096]{1,0:T(8,128)(2,1)}, bf16[512,4096]{1,0:T(8,128)(2,1)}) fusion(f32[4096]{0:T(1024)S(1)} %select_multiply_fusion, s32[512]{0:T(512)S(1)} %iota_add_fusion), kind=kLoop, calls=%fused_computation.11 | loop fusion | flops 39845888 | bytes 8407040 | tf_op jit(solution)/shard_map/convert.1
  49.5 0.0 all-to-all-done
  49.6 0.3 reduce_sum.156
  49.9 0.0 copy-start
  50.0 1.2 %add_convert_fusion = (bf16[2,8,16,4096]{3,2,1,0:T(8,128)(2,1)S(1)}, bf16[2,8,16,4096]{3,2,1,0:T(8,128)(2,1)S(1)}) fusion(f32[2,16,4096]{2,1,0:T(8,128)S(1)} %get-tuple-element.18, f32[2,8,4096]{2,1,0:T(8,128)S(1)} %get-tuple-element.20, f32[2,16,4096]{2,1,0:T(8,128)S(1)} %get-tuple-element.17, f32[2,8,4096]{2,1,0:T(8,128)S(1)} %get-tuple-element.19), kind=kLoop, calls=%fused_computation.21 | loop fusion | flops 8388608 | bytes 5767168 | tf_op jit(solution)/shard_map/convert.6
  51.2 0.9 copy-done
  52.1 4.9 %fusion.13 = f32[2,512,128]{1,2,0:T(8,128)S(1)} fusion(bf16[512,4096]{1,0:T(8,128)(2,1)} %get-tuple-element.22, bf16[512,4096]{1,0:T(8,128)(2,1)S(1)} %copy-done, bf16[2,128,4096]{2,1,0:T(8,128)(2,1)S(1)} %bitcast.100, bf16[2,128,4096]{2,1,0:T(8,128)(2,1)S(1)} %bitcast.99), kind=kOutput, calls=%fused_computation.22 | convolution fusion | flops 2172649472 | bytes 13107200 | tf_op jit(solution)/shard_map/lk,wpk->wlp/dot_general | solution.py:75
  57.0 0.2 copy.6
  57.3 44.9 %all_to_all.20 = f32[2,512,128]{2,0,1:T(2,128)S(1)} all-to-all(f32[2,512,128]{2,0,1:T(2,128)S(1)} %copy.6), channel_id=1, replica_groups=mesh['win'=64,'rcv'=8] {'win'}, dimensions={1} | all-to-all | bytes 1048576 | tf_op jit(solution)/shard_map/all_to_all | solution.py:77
  102.1 0.1 bitcast_reduce_fusion
  102.3 0.1 fusion.30
  102.4 0.2 fusion.31
  102.6 0.1 fusion.29
  102.8 0.2 fusion.32
  103.0 0.1 fusion.28
  103.1 0.2 fusion.33
  103.3 0.1 fusion.27
  103.5 0.2 fusion.34
  103.7 0.1 fusion.26
  103.8 0.2 fusion.35
  104.0 0.7 div.134
  (16 shorter events, 0.2 us)
Async XLA Ops:
  0.0 13.4 %copy-start.1 = (bf16[2,2,16,4096]{3,2,1,0:T(8,128)(2,1)S(1)}, bf16[2,2,16,4096]{3,2,1,0:T(8,128)(2,1)}, u32[]{:S(2)}) copy-start(bf16[2,2,16,4096]{3,2,1,0:T(8,128)(2,1)} %param.2) | copy-start | bytes 1572868
  3.0 46.5 %all-to-all-start = ((bf16[8,2,2,8,4096]{4,3,2,1,0:T(8,128)(2,1)}), bf16[8,2,2,8,4096]{4,3,2,1,0:T(8,128)(2,1)S(1)}, u32[]{:S(2)}, u32[]{:S(2)}) async-start(bf16[8,2,2,8,4096]{4,3,2,1,0:T(8,128)(2,1)} %broadcast_in_dim.18), calls=%async_computation | async-start | bytes 4194304 | tf_op jit(solution)/shard_map/all_to_all | solution.py:16
  49.9 2.2 %copy-start = (bf16[512,4096]{1,0:T(8,128)(2,1)S(1)}, bf16[512,4096]{1,0:T(8,128)(2,1)}, u32[]{:S(2)}) copy-start(bf16[512,4096]{1,0:T(8,128)(2,1)} %get-tuple-element.21) | copy-start | bytes 12582916
where the time goes:
time: 106 us; the launch traced here: 105 us
  blocking collectives  44.9 us (42%)
  other arithmetic  39.4 us (37%)
  starting transfers between devices  10.3 us (10%)
  matrix products  6.31 us (6%)
  local copies, waits for them, and re-layouts  3.59 us (3%)
    all_to_all x1, blocking collectives, per_device(): lax.all_to_all(corr, 'win', split_axis=1, concat_axis=0, tiled=True)  44.9 us
    another operation x2, other arithmetic  37.2 us
    all_to_all x1, starting transfers between devices, copy_for_each(): lax.all_to_all(jnp.broadcast_to(value[None], (length, *value.shape)), axi...  10.3 us
    dot_general x1, matrix products, per_device(): jnp.einsum('lk,wpk->wlp', basis, cross, preferred_element_type=jnp.float32)  4.93 us
  transfers between devices with their start and end apart: 1, of which 0 were waited for; matrix products, arithmetic and copies ran while one was open for 35% of the time, Pallas kernels for 0%

commit v1 on v0

v1 whole, which is shorter than its diff:
```python
import jax
import jax.numpy as jnp
from jax import lax
from jax.experimental import pallas as pl
from jax.experimental.pallas import tpu as pltpu
from jax.sharding import PartitionSpec as P

L = 512
ITERS = 5
TUKEY = 4.685
EPSILON = 1e-06
MESH = pl.DeviceIdType.MESH
NZ, NX = 16, 4
WIN = NZ * NX
BLOCK = L // WIN


def signed(step, count):
    return step if step <= count // 2 else step - count


def offsets():
    found = [(dz, dx) for dz in range(NZ) for dx in range(NX) if dz or dx]
    return sorted(found, key=lambda o: -(4 * abs(signed(o[0], NZ)) + abs(signed(o[1], NX))))


def tables(shifts, bins, total):
    angle = (shifts[:, None] * bins[None, :] % total).astype(jnp.float32) * (2.0 * jnp.pi / total)
    return jnp.cos(angle), jnp.sin(angle)


def make_basis(bin_count):
    freq = jnp.arange(bin_count, dtype=jnp.int32)
    total = 2 * bin_count
    factor = jnp.where(freq == 0, 1.0, 2.0).astype(jnp.float32) / jnp.sqrt(jnp.float32(4 * total))
    coarse_c, coarse_s = tables(jnp.arange(32, dtype=jnp.int32) * 16 - L // 2, freq, total)
    fine_c, fine_s = tables(jnp.arange(16, dtype=jnp.int32), freq, total)
    coarse_c, coarse_s, fine_c, fine_s = lax.optimization_barrier((coarse_c * factor, coarse_s * factor, fine_c, fine_s))
    cos = coarse_c[:, None] * fine_c[None] - coarse_s[:, None] * fine_s[None]
    sin = coarse_s[:, None] * fine_c[None] + coarse_c[:, None] * fine_s[None]
    return cos.astype(jnp.bfloat16).reshape(L, bin_count), (-sin).astype(jnp.bfloat16).reshape(L, bin_count)


def stack_kernel(x_ref, o_ref, got, vals, send_sem, recv_sem):
    me = lax.axis_index("win")
    z, x = me // NX, lax.rem(me, NX)
    peers = [lax.rem(z + dz, NZ) * NX + lax.rem(x + dx, NX) for dz, dx in offsets()]
    barrier = pltpu.get_barrier_semaphore()
    for peer in peers:
        pl.semaphore_signal(barrier, inc=1, device_id={"win": peer}, device_id_type=MESH)
    pl.semaphore_wait(barrier, WIN - 1)
    for peer in peers:
        pltpu.make_async_remote_copy(
            x_ref.at[peer], got.at[me], send_sem, recv_sem, device_id={"win": peer}, device_id_type=MESH
        ).start()
    got[me] = x_ref[me]
    pltpu.make_async_copy(got.at[pl.ds(0, WIN - 1)], got.at[pl.ds(0, WIN - 1)], recv_sem).wait()
    windows = 2 * WIN
    sums = [None] * 8
    for w in range(windows):
        value = got[w // 2, pl.ds(BLOCK * (w % 2), BLOCK), :].astype(jnp.float32) * (1.0 / (1.0 + w / 128.0))
        vals[w] = value
        sums[w % 8] = value if sums[w % 8] is None else sums[w % 8] + value
    total = sum(sums[1:], sums[0])
    mean = total * (1.0 / windows)
    sums = [jnp.zeros_like(mean)] * 8
    for w in range(windows):
        dev = vals[w] - mean
        sums[w % 8] = sums[w % 8] + dev * dev
    var = sum(sums[1:], sums[0]) * (1.0 / windows)
    center = mean
    for _ in range(ITERS):
        shift = mean - center
        inverse = 1.0 / (TUKEY * TUKEY * (var + shift * shift + EPSILON))
        weights = [jnp.zeros_like(mean)] * 8
        moved = [jnp.zeros_like(mean)] * 8
        for w in range(windows):
            dev = vals[w] - center
            root = jnp.maximum(1.0 - dev * dev * inverse, 0.0)
            weight = root * root
            weights[w % 8] = weights[w % 8] + weight
            moved[w % 8] = moved[w % 8] + weight * dev
        center = center + sum(moved[1:], moved[0]) / sum(weights[1:], weights[0])
    o_ref[...] = center
    pltpu.make_async_copy(x_ref.at[pl.ds(0, WIN - 1)], x_ref.at[pl.ds(0, WIN - 1)], send_sem).wait()


def exchange_and_stack(blocks):
    return pl.pallas_call(
        stack_kernel,
        out_shape=jax.ShapeDtypeStruct((BLOCK, 128), jnp.float32),
        in_specs=[pl.BlockSpec(memory_space=pltpu.VMEM)],
        out_specs=pl.BlockSpec(memory_space=pltpu.VMEM),
        scratch_shapes=[
            pltpu.VMEM((WIN, 2 * BLOCK, 128), jnp.bfloat16),
            pltpu.VMEM((2 * WIN, BLOCK, 128), jnp.float32),
            pltpu.SemaphoreType.DMA,
            pltpu.SemaphoreType.DMA,
        ],
        compiler_params=pltpu.CompilerParams(collective_id=0, has_side_effects=True),
    )(blocks)


def per_device(spectra, source_channel):
    win_count, _, chan_count, bin_count = spectra.shape
    source_count = source_channel.shape[0]
    channels = lax.axis_index("rcv") * chan_count + lax.iota(jnp.int32, chan_count)
    onehot = (source_channel[:, None] == channels[None, :]).astype(jnp.bfloat16)
    own_part = jnp.einsum("sr,wcrf->wcsf", onehot, spectra, preferred_element_type=jnp.float32).astype(jnp.bfloat16)
    parts = lax.all_to_all(jnp.broadcast_to(own_part[None], (8, *own_part.shape)), "rcv", 0, 0, tiled=True)
    source_float = parts.astype(jnp.float32).sum(axis=0)
    receiver_float = spectra.astype(jnp.float32)
    real_a = source_float[:, 0][:, :, None, :]
    imag_b = source_float[:, 1][:, :, None, :]
    real_p = receiver_float[:, 0][:, None, :, :]
    imag_q = receiver_float[:, 1][:, None, :, :]
    pair_count = source_count * chan_count
    real_part = (real_a * real_p + imag_b * imag_q).reshape(win_count, pair_count, bin_count).astype(jnp.bfloat16)
    imag_part = (imag_b * real_p - real_a * imag_q).reshape(win_count, pair_count, bin_count).astype(jnp.bfloat16)
    cos, sin = make_basis(bin_count)
    corr = jnp.einsum("lk,wpk->lwp", cos, real_part, preferred_element_type=jnp.float32)
    corr = corr + jnp.einsum("lk,wpk->lwp", sin, imag_part, preferred_element_type=jnp.float32)
    window = 2 * lax.axis_index("win") + lax.iota(jnp.int32, 2)
    scaled = corr * (1.0 + window.astype(jnp.float32) / 128.0)[None, :, None]
    blocks = scaled.astype(jnp.bfloat16).reshape(WIN, BLOCK, 2, pair_count).transpose(0, 2, 1, 3)
    result = exchange_and_stack(blocks.reshape(WIN, 2 * BLOCK, pair_count))
    return result.reshape(BLOCK, source_count, chan_count)


def solution(mesh):
    return jax.shard_map(
        per_device,
        mesh=mesh,
        in_specs=(P("win", None, "rcv", None), P()),
        out_specs=P("win", None, "rcv"),
        check_vma=False,
    )
```

time: 106 us -> 75.6 us (0.71)
  blocking collectives: 44.9 us -> 0 us
  Pallas kernels: 0 us -> 27.9 us
  other arithmetic: 39.4 us -> 12.5 us
  waiting for transfers between devices: 0.01 us -> 14.2 us
  local copies, waits for them, and re-layouts: 3.59 us -> 6.31 us
  matrix products: 6.31 us -> 3.9 us
    all_to_all x1 -> x0, blocking collectives: 44.9 us -> none  [per_device(): lax.all_to_all(corr, 'win', split_axis=1, concat_axis=0, tiled=True)]
    another operation x2 -> x0, other arithmetic: 37.2 us -> none
    pallas_call x0 -> x1, Pallas kernels: none -> 27.9 us  [exchange_and_stack(): pl.pallas_call(stack_kernel, out_shape=jax.ShapeDtypeStruct((BLOCK, 128),...]
    all_to_all x1, waiting for transfers between devices: 0.01 us -> 14.2 us  [per_device(): lax.all_to_all(jnp.broadcast_to(own_part[None], (8, *own_part.shape)), 'r...]
    convert_element_type x1 -> x2, other arithmetic: 0.04 us -> 7.24 us  [the longest x1 6 us: make_basis(): (-sin).astype(jnp.bfloat16).reshape(L, bin_count)]
    dot_general x1 -> x2, matrix products: 4.93 us -> 2.57 us  [the longest x1 1.29 us: per_device(): jnp.einsum('lk,wpk->lwp', sin, imag_part, preferred_element_type=jnp.floa...]
    reshape x0 -> x2, local copies, waits for them, and re-layouts: none -> 2.12 us  [the longest x1 1.37 us: per_device(): return result.reshape(BLOCK, source_count, chan_count)]
    mul x5 -> x1, other arithmetic: 0.04 us -> 2.15 us  [make_basis(): coarse_s * factor]
  transfers between devices with their start and end apart: 1 -> 1, of which waited for: 0 -> 1; matrix products, arithmetic and copies ran while one was open for 35% -> 16% of each run, Pallas kernels for 0% -> 0%
where the time goes in v1:
time: 75.6 us; the launch traced here: 75.2 us
  Pallas kernels  27.9 us (37%)
  waiting for transfers between devices  14.2 us (19%)
  other arithmetic  12.5 us (17%)
  starting transfers between devices  10.3 us (14%)
  local copies, waits for them, and re-layouts  6.31 us (8%)
  matrix products  3.9 us (5%)
    pallas_call x1, Pallas kernels, exchange_and_stack(): pl.pallas_call(stack_kernel, out_shape=jax.ShapeDtypeStruct((BLOCK, 128),...  27.9 us
    all_to_all x1, waiting for transfers between devices, per_device(): lax.all_to_all(jnp.broadcast_to(own_part[None], (8, *own_part.shape)), 'r...  14.2 us
    all_to_all x1, starting transfers between devices, per_device(): lax.all_to_all(jnp.broadcast_to(own_part[None], (8, *own_part.shape)), 'r...  10.3 us
    convert_element_type x1, other arithmetic, make_basis(): (-sin).astype(jnp.bfloat16).reshape(L, bin_count)  6 us
    mul x1, other arithmetic, make_basis(): coarse_s * factor  2.15 us
    sin x1, other arithmetic, tables(): return (jnp.cos(angle), jnp.sin(angle))  1.73 us
    broadcast_in_dim x1, local copies, waits for them, and re-layouts, per_device(): jnp.broadcast_to(own_part[None], (8, *own_part.shape))  1.61 us
  transfers between devices with their start and end apart: 1, of which 1 were waited for; matrix products, arithmetic and copies ran while one was open for 16% of the time, Pallas kernels for 0%

profile of v1, /device:TPU:1, one launch (start us, length us, event | category | flops | bytes accessed | tf_op | source)
XLA Modules:
  0.0 75.2 jit_solution(4081308264101354139)
XLA Ops:
  0.0 1.3 %fusion = bf16[2,2,8,4096]{3,2,1,0:T(8,128)(2,1)S(1)} fusion(bf16[2,2,16,4096]{3,2,1,0:T(8,128)(2,1)} %param.2, s32[16]{0:T(128)S(1)} %iota_add_fusion, s32[8]{0:T(128)} %param.3), kind=kOutput, calls=%fused_computation.3 | convolution fusion | flops 4325504 | bytes 786528 | tf_op jit(solution)/shard_map/sr,wcrf->wcsf/dot_general | solution.py:109
  1.3 1.6 %broadcast_in_dim.12 = bf16[8,2,2,8,4096]{4,3,2,1,0:T(8,128)(2,1)} broadcast(bf16[2,2,8,4096]{3,2,1,0:T(8,128)(2,1)S(1)} %fusion), dimensions={1,2,3,4} | broadcast | bytes 2359296 | tf_op jit(solution)/shard_map/broadcast_in_dim | solution.py:110
  2.9 10.3 %all-to-all-start = ((bf16[8,2,2,8,4096]{4,3,2,1,0:T(8,128)(2,1)}), bf16[8,2,2,8,4096]{4,3,2,1,0:T(8,128)(2,1)S(1)}, u32[]{:S(2)}, u32[]{:S(2)}) async-start(bf16[8,2,2,8,4096]{4,3,2,1,0:T(8,128)(2,1)} %broadcast_in_dim.12), calls=%async_computation | async-start | bytes 4194304 | tf_op jit(solution)/shard_map/all_to_all | solution.py:110
  13.3 1.7 %fusion.16 = (f32[16,4096]{1,0:T(8,128)S(1)}, f32[16,4096]{1,0:T(8,128)}) fusion(), kind=kLoop, calls=%fused_computation.36 | loop fusion | flops 917504 | bytes 524288 | tf_op jit(solution)/shard_map/sin | solution.py:29
  15.0 1.1 %convert_element_type.90 = f32[2,2,16,4096]{3,2,1,0:T(8,128)S(1)} convert(bf16[2,2,16,4096]{3,2,1,0:T(8,128)(2,1)} %param.2) | non-fusion elementwise | flops 262144 | bytes 1572864 | tf_op jit(solution)/shard_map/convert_element_type | solution.py:112
  16.2 2.1 %sine_multiply_fusion = (f32[32,4096]{1,0:T(8,128)S(1)}, f32[32,4096]{1,0:T(8,128)S(1)}) fusion(f32[4096]{0:T(1024)S(1)} %select_multiply_fusion, s32[32]{0:T(128)S(1)} %multiply_add_fusion.1), kind=kLoop, calls=%fused_computation.19 | loop fusion | flops 2097152 | bytes 1065088 | tf_op jit(solution)/shard_map/mul | solution.py:38
  18.3 1.1 %slice_bitcast_fusion.1 = (f32[2,16,4096]{2,1,0:T(8,128)}, f32[2,16,4096]{2,1,0:T(8,128)}) fusion(f32[2,2,16,4096]{3,2,1,0:T(8,128)S(1)} %convert_element_type.90), kind=kLoop, calls=%fused_computation.18 | loop fusion | bytes 2097152 | tf_op jit(solution)/shard_map/mul | solution.py:118
  19.4 0.0 copy-start.2
  19.4 0.0 copy-start.3
  19.4 6.0 %negate_convert_fusion = (bf16[32,16,4096]{2,1,0:T(8,128)(2,1)}, bf16[32,16,4096]{2,1,0:T(8,128)(2,1)}) fusion(f32[16,4096]{1,0:T(8,128)S(1)} %get-tuple-element.12, f32[32,4096]{1,0:T(8,128)S(1)} %get-tuple-element.11, f32[16,4096]{1,0:T(8,128)} %get-tuple-element.10, f32[32,4096]{1,0:T(8,128)S(1)} %get-tuple-element.9), kind=kLoop, calls=%fused_computation | loop fusion | flops 18874368 | bytes 9961472 | tf_op jit(solution)/shard_map/convert_element_type | solution.py:41
  25.4 14.2 %all-to-all-done = bf16[8,2,2,8,4096]{4,3,2,1,0:T(8,128)(2,1)S(1)} async-done(((bf16[8,2,2,8,4096]{4,3,2,1,0:T(8,128)(2,1)}), bf16[8,2,2,8,4096]{4,3,2,1,0:T(8,128)(2,1)S(1)}, u32[]{:S(2)}, u32[]{:S(2)}) %all-to-all-start) | async-done | bytes 2097184 | tf_op jit(solution)/shard_map/all_to_all | solution.py:110
  39.5 0.0 copy-start.1
  39.5 0.3 convert_reduce_fusion
  39.9 0.0 copy-done.2
  39.9 0.0 copy-done.3
  39.9 1.2 %subtract_convert_fusion.1 = (bf16[2,8,16,4096]{3,2,1,0:T(8,128)(2,1)S(1)}, bf16[2,8,16,4096]{3,2,1,0:T(8,128)(2,1)S(1)}) fusion(f32[2,16,4096]{2,1,0:T(8,128)S(1)} %copy-done.3, f32[2,8,4096]{2,1,0:T(8,128)S(1)} %get-tuple-element.20, f32[2,16,4096]{2,1,0:T(8,128)S(1)} %copy-done.2, f32[2,8,4096]{2,1,0:T(8,128)S(1)} %get-tuple-element.19), kind=kLoop, calls=%fused_computation.4 | loop fusion | flops 8388608 | bytes 5767168 | tf_op jit(solution)/shard_map/convert_element_type | solution.py:119
  41.1 0.6 copy-done.1
  41.7 0.0 copy-start
  41.7 1.3 %fusion.22 = f32[512,2,128]{2,0,1:T(8,128)S(1)} fusion(bf16[512,4096,1]{1,0,2:T(8,128)(2,1)S(1)} %bitcast.36, bf16[2,128,4096]{2,1,0:T(8,128)(2,1)S(1)} %bitcast.38), kind=kOutput, calls=%fused_computation.47 | convolution fusion | flops 1073741824 | bytes 6815744 | tf_op jit(solution)/shard_map/lk,wpk->lwp/dot_general | solution.py:121
  43.0 0.9 %copy-done = bf16[32,16,4096]{2,1,0:T(8,128)(2,1)S(1)} copy-done((bf16[32,16,4096]{2,1,0:T(8,128)(2,1)S(1)}, bf16[32,16,4096]{2,1,0:T(8,128)(2,1)}, u32[]{:S(2)}) %copy-start) | copy-done | bytes 4194328
  43.9 1.3 %fusion.3 = bf16[64,8,2,128]{3,1,0,2:T(8,128)(2,1)S(1)} fusion(f32[512,2,128]{2,0,1:T(8,128)S(1)} %fusion.22, bf16[512,4096,1]{1,0,2:T(8,128)(2,1)S(1)} %bitcast.35, bf16[2,128,4096]{2,1,0:T(8,128)(2,1)S(1)} %bitcast.37, f32[2]{0:T(128)S(1)} %multiply_add_fusion), kind=kOutput, calls=%fused_computation.10 | convolution fusion | flops 1074135040 | bytes 7077896 | tf_op jit(solution)/shard_map/lk,wpk->lwp/dot_general | solution.py:122
  45.2 0.7 copy.7
  45.9 27.9 %shard_map.28 = f32[8,128]{1,0:T(8,128)} custom-call(bf16[64,16,128]{2,1,0:T(8,128)(2,1)} %bitcast.39), custom_call_target="tpu_custom_call" | custom-call | tf_op jit(solution)/shard_map/pallas_call | solution.py:89
  73.8 1.4 %reshape.125 = f32[8,8,16]{2,1,0:T(8,128)} reshape(f32[8,128]{1,0:T(8,128)} %shard_map.28) | data formatting | bytes 8192 | tf_op jit(solution)/shard_map/reshape | solution.py:127
  (5 shorter events, 0.1 us)
Async XLA Ops:
  2.9 36.6 %all-to-all-start = ((bf16[8,2,2,8,4096]{4,3,2,1,0:T(8,128)(2,1)}), bf16[8,2,2,8,4096]{4,3,2,1,0:T(8,128)(2,1)S(1)}, u32[]{:S(2)}, u32[]{:S(2)}) async-start(bf16[8,2,2,8,4096]{4,3,2,1,0:T(8,128)(2,1)} %broadcast_in_dim.12), calls=%async_computation | async-start | bytes 4194304 | tf_op jit(solution)/shard_map/all_to_all | solution.py:110
  19.4 20.5 %copy-start.2 = (f32[2,16,4096]{2,1,0:T(8,128)S(1)}, f32[2,16,4096]{2,1,0:T(8,128)}, u32[]{:S(2)}) copy-start(f32[2,16,4096]{2,1,0:T(8,128)} %get-tuple-element.17) | copy-start | bytes 1572868
  19.4 20.5 %copy-start.3 = (f32[2,16,4096]{2,1,0:T(8,128)S(1)}, f32[2,16,4096]{2,1,0:T(8,128)}, u32[]{:S(2)}) copy-start(f32[2,16,4096]{2,1,0:T(8,128)} %get-tuple-element.18) | copy-start | bytes 1572868
  39.5 2.2 %copy-start.1 = (bf16[32,16,4096]{2,1,0:T(8,128)(2,1)S(1)}, bf16[32,16,4096]{2,1,0:T(8,128)(2,1)}, u32[]{:S(2)}) copy-start(bf16[32,16,4096]{2,1,0:T(8,128)(2,1)} %get-tuple-element.16) | copy-start | bytes 12582916
  41.7 2.2 %copy-start = (bf16[32,16,4096]{2,1,0:T(8,128)(2,1)S(1)}, bf16[32,16,4096]{2,1,0:T(8,128)(2,1)}, u32[]{:S(2)}) copy-start(bf16[32,16,4096]{2,1,0:T(8,128)(2,1)} %get-tuple-element.15) | copy-start | bytes 12582916

commit v2 on v1

v2 whole, which is shorter than its diff:
```python
import jax
import jax.numpy as jnp
from jax import lax
from jax.experimental import pallas as pl
from jax.experimental.pallas import tpu as pltpu
from jax.sharding import PartitionSpec as P

L = 512
F = 4096
ITERS = 5
TUKEY = 4.685
EPSILON = 1e-06
MESH = pl.DeviceIdType.MESH
NZ, NX, NY = 16, 4, 4
WIN = NZ * NX
BLOCK = L // WIN
HALF = L // 2
ROWS = HALF + 16
QUARTER = F // NY
COLS = 512
PAIRS = 128


def signed(step, count):
    return step if step <= count // 2 else step - count


def offsets():
    found = [(dz, dx) for dz in range(NZ) for dx in range(NX) if dz or dx]
    return sorted(found, key=lambda o: -(4 * abs(signed(o[0], NZ)) + abs(signed(o[1], NX))))


def cos_sin(phase):
    turn = (phase + 1024) >> 11
    x = (phase - (turn << 11)).astype(jnp.float32) * (2.0 * jnp.pi / (2 * F))
    y = x * x
    s = x * (1.0 + y * (-1.0 / 6 + y * (1.0 / 120 + y * (-1.0 / 5040 + y * (1.0 / 362880)))))
    c = 1.0 + y * (-0.5 + y * (1.0 / 24 + y * (-1.0 / 720 + y * (1.0 / 40320))))
    odd = (turn & 1) == 1
    cos = jnp.where(odd, s, c)
    sin = jnp.where(odd, c, s)
    cos = jnp.where(((turn + 1) & 2) == 2, -cos, cos)
    sin = jnp.where((turn & 2) == 2, -sin, sin)
    return cos, sin


def fill_table(cos_ref, sin_ref, rows, step, scaled):
    for part in range(F // COLS):
        cols = pl.ds(part * COLS, COLS)
        freq = part * COLS + lax.broadcasted_iota(jnp.int32, (rows, COLS), 1)
        row = lax.broadcasted_iota(jnp.int32, (rows, COLS), 0)
        cos, sin = cos_sin((row * freq * step) & (2 * F - 1))
        if scaled:
            factor = jnp.where(freq == 0, 1.0, 2.0) * (1.0 / (8 * F) ** 0.5)
            cos, sin = cos * factor, sin * factor
        cos_ref[:, cols] = cos
        sin_ref[:, cols] = sin


def fill_basis(first, last, coarse_c, coarse_s, fine_c, fine_s, basis_c, basis_s):
    for part in range(F // COLS):
        cols = pl.ds(part * COLS, COLS)
        quarter, start = divmod(part * COLS, QUARTER)
        fc, fs = fine_c[:, cols], fine_s[:, cols]

        def one(g, _, cols=cols, quarter=quarter, start=start, fc=fc, fs=fs):
            cc, cs = coarse_c[pl.ds(g, 1), cols], coarse_s[pl.ds(g, 1), cols]
            rows = pl.ds(pl.multiple_of(g * 16, 16), 16)
            basis_c[quarter, rows, start : start + COLS] = (cc * fc - cs * fs).astype(jnp.bfloat16)
            basis_s[quarter, rows, start : start + COLS] = (-(cs * fc) - cc * fs).astype(jnp.bfloat16)
            return 0

        lax.fori_loop(first, last, one, 0)


def stack(got, vals):
    windows = 2 * WIN
    sums = [None] * 8
    for w in range(windows):
        value = got[w // 2, pl.ds(BLOCK * (w % 2), BLOCK), :].astype(jnp.float32) * (1.0 / (1.0 + w / 128.0))
        vals[w] = value
        sums[w % 8] = value if sums[w % 8] is None else sums[w % 8] + value
    total = sum(sums[1:], sums[0])
    mean = total * (1.0 / windows)
    sums = [jnp.zeros_like(mean)] * 8
    for w in range(windows):
        dev = vals[w] - mean
        sums[w % 8] = sums[w % 8] + dev * dev
    var = sum(sums[1:], sums[0]) * (1.0 / windows)
    center = mean
    for _ in range(ITERS):
        shift = mean - center
        inverse = 1.0 / (TUKEY * TUKEY * (var + shift * shift + EPSILON))
        weights = [jnp.zeros_like(mean)] * 8
        moved = [jnp.zeros_like(mean)] * 8
        for w in range(windows):
            dev = vals[w] - center
            root = jnp.maximum(1.0 - dev * dev * inverse, 0.0)
            weight = root * root
            weights[w % 8] = weights[w % 8] + weight
            moved[w % 8] = moved[w % 8] + weight * dev
        center = center + sum(moved[1:], moved[0]) / sum(weights[1:], weights[0])
    return center


def remote(src, dst, send_sem, recv_sem, where):
    return pltpu.make_async_remote_copy(src, dst, send_sem, recv_sem, device_id=where, device_id_type=MESH)


def wait_bytes(ref, sem):
    pltpu.make_async_copy(ref, ref, sem).wait()


def kernel(
    channel_ref, spectra_ref, o_ref,
    spec, own, pair, summed, parts, sources, source_f,
    coarse_c, coarse_s, fine_c, fine_s, basis_c, basis_s, cross_r, cross_i, acc_c, acc_s,
    blocks, got, vals,
    spec_sem, pair_s, pair_r, part_s, part_r, all_s, all_r, to_s, to_r, send_s, send_r,
):
    me = lax.axis_index("win")
    z, x = me // NX, lax.rem(me, NX)
    mine = lax.axis_index("rcv")
    y, core = mine // 2, lax.rem(mine, 2)
    other = 1 - core
    peers = [lax.rem(z + dz, NZ) * NX + lax.rem(x + dx, NX) for dz, dx in offsets()]
    partner = {"rcv": 2 * y + other}
    across = {d: {"rcv": 2 * lax.rem(y + d, NY) + core} for d in (1, 2, 3)}
    quarter = {d: lax.rem(y + NY - d, NY) for d in range(NY)}

    loads = [
        pltpu.make_async_copy(spectra_ref.at[:, :, :, pl.ds(q * QUARTER, QUARTER)], spec.at[q], spec_sem.at[q])
        for q in range(NY)
    ]
    for load in loads:
        load.start()
    barrier = pltpu.get_barrier_semaphore()
    for d in range(1, 8):
        pl.semaphore_signal(barrier, inc=1, device_id={"rcv": lax.rem(mine + d, 8)}, device_id_type=MESH)
    for peer in peers:
        pl.semaphore_signal(barrier, inc=1, device_id={"win": peer}, device_id_type=MESH)

    fill_table(fine_c, fine_s, 16, 1, False)
    for load in loads:
        load.wait()
    row = lax.broadcasted_iota(jnp.int32, (16, 16), 0)
    column = lax.broadcasted_iota(jnp.int32, (16, 16), 1) + mine * 16
    onehot = jnp.zeros((16, 16), jnp.float32)
    for s in range(8):
        onehot = jnp.where((row == s) & (column == channel_ref[s]), 1.0, onehot)
    onehot = onehot.astype(jnp.bfloat16)
    for w in range(2):
        for q in range(NY):
            picked = [
                jnp.dot(onehot, spec[q, w, c], preferred_element_type=jnp.float32)[:8] for c in range(2)
            ]
            own[w, q] = jnp.concatenate(picked, axis=0).astype(jnp.bfloat16)
    pl.semaphore_wait(barrier, 7 + WIN - 1)

    swap = remote(own.at[other], pair, pair_s, pair_r, partner)
    swap.start()
    fill_table(coarse_c, coarse_s, 24, 16, True)
    swap.wait_recv()
    for q in range(NY):
        summed[q] = own[core, q] + pair[q]
    scatter = [
        remote(summed.at[lax.rem(y + d, NY)], parts.at[d - 1], part_s, part_r, across[d]) for d in (2, 1, 3)
    ]
    for copy in scatter:
        copy.start()
    fill_basis(0, ROWS // 16, coarse_c, coarse_s, fine_c, fine_s, basis_c, basis_s)
    wait_bytes(parts, part_r)
    sources[core, y] = summed[y] + parts[0] + parts[1] + parts[2]
    held = sources.at[core, y]
    gather = {d: remote(held, held, all_s, all_r.at[d - 1], across[d]) for d in (2, 1, 3)}
    for d in (2, 1, 3):
        gather[d].start()

    def hand(d):
        there = sources.at[core, quarter[d]]
        copy = remote(there, there, to_s, to_r.at[d], partner)
        copy.start()
        return copy

    def compute(d):
        q = quarter[d]
        hands[d].wait_recv()
        for w in range(2):
            source_f[w] = sources[w, q].astype(jnp.float32)
        for w in range(2):
            for part in range(QUARTER // COLS):
                cols = pl.ds(part * COLS, COLS)
                p = spec[q, w, 0, :, cols].astype(jnp.float32)
                i = spec[q, w, 1, :, cols].astype(jnp.float32)
                for s in range(8):
                    a = source_f[w, pl.ds(s, 1), cols]
                    b = source_f[w, pl.ds(8 + s, 1), cols]
                    rows = pl.ds(w * PAIRS + s * 16, 16)
                    cross_r[d, rows, cols] = (a * p + b * i).astype(jnp.bfloat16)
                    cross_i[d, rows, cols] = (b * p - a * i).astype(jnp.bfloat16)
        dims = (((1,), (1,)), ((), ()))
        sum_c = lax.dot_general(basis_c[q], cross_r[d], dims, preferred_element_type=jnp.float32)
        sum_s = lax.dot_general(basis_s[q], cross_i[d], dims, preferred_element_type=jnp.float32)
        if d == 0:
            acc_c[...] = sum_c
            acc_s[...] = sum_s
        else:
            acc_c[...] += sum_c
            acc_s[...] += sum_s

    hands = {0: hand(0)}
    compute(0)
    for d in (1, 3, 2):
        gather[d].wait_recv()
        hands[d] = hand(d)
    for d in (1, 3, 2):
        compute(d)

    window = (2 * me).astype(jnp.float32)
    scales = [1.0 + (window + w) * (1.0 / 128.0) for w in range(2)]
    for ahead in (True, False):
        first = 0 if ahead else 1
        c, s = acc_c[pl.ds(first, HALF), :], acc_s[pl.ds(first, HALF), :]
        lags = c + s if ahead else c - s
        halves = [(lags[:, w * PAIRS : (w + 1) * PAIRS] * scales[w]).reshape(32, BLOCK, PAIRS) for w in range(2)]
        both = jnp.concatenate(halves, axis=1).astype(jnp.bfloat16)
        if ahead:
            blocks[pl.ds(32, 32)] = both
        else:
            for m in range(32):
                blocks[31 - m] = both[m]
    for peer in peers:
        remote(blocks.at[peer], got.at[me], send_s, send_r, {"win": peer}).start()
    got[me] = blocks[me]
    wait_bytes(got.at[pl.ds(0, WIN - 1)], send_r)
    center = stack(got, vals)

    @pl.when(me >= 32)
    def _():
        o_ref[...] = center

    @pl.when(me < 32)
    def _():
        for k in range(BLOCK):
            o_ref[pl.ds(BLOCK - 1 - k, 1), :] = center[k : k + 1]

    swap.wait_send()
    wait_bytes(parts, part_s)
    wait_bytes(parts, all_s)
    wait_bytes(sources.at[0], to_s)
    wait_bytes(blocks.at[pl.ds(0, WIN - 1)], send_s)


def per_device(spectra, source_channel):
    bf, f32, dma = jnp.bfloat16, jnp.float32, pltpu.SemaphoreType.DMA
    result = pl.pallas_call(
        kernel,
        out_shape=jax.ShapeDtypeStruct((BLOCK, PAIRS), f32),
        in_specs=[pl.BlockSpec(memory_space=pltpu.SMEM), pl.BlockSpec(memory_space=pl.ANY)],
        out_specs=pl.BlockSpec(memory_space=pltpu.VMEM),
        scratch_shapes=[
            pltpu.VMEM((NY, 2, 2, 16, QUARTER), bf),
            pltpu.VMEM((2, NY, 16, QUARTER), bf),
            pltpu.VMEM((NY, 16, QUARTER), bf),
            pltpu.VMEM((NY, 16, QUARTER), bf),
            pltpu.VMEM((NY - 1, 16, QUARTER), bf),
            pltpu.VMEM((2, NY, 16, QUARTER), bf),
            pltpu.VMEM((2, 16, QUARTER), f32),
            pltpu.VMEM((24, F), f32),
            pltpu.VMEM((24, F), f32),
            pltpu.VMEM((16, F), f32),
            pltpu.VMEM((16, F), f32),
            pltpu.VMEM((NY, ROWS, QUARTER), bf),
            pltpu.VMEM((NY, ROWS, QUARTER), bf),
            pltpu.VMEM((NY, 2 * PAIRS, QUARTER), bf),
            pltpu.VMEM((NY, 2 * PAIRS, QUARTER), bf),
            pltpu.VMEM((ROWS, 2 * PAIRS), f32),
            pltpu.VMEM((ROWS, 2 * PAIRS), f32),
            pltpu.VMEM((WIN, 2 * BLOCK, PAIRS), bf),
            pltpu.VMEM((WIN, 2 * BLOCK, PAIRS), bf),
            pltpu.VMEM((2 * WIN, BLOCK, PAIRS), f32),
            dma((NY,)), dma, dma, dma, dma, dma, dma((NY - 1,)), dma, dma((NY,)), dma, dma,
        ],
        compiler_params=pltpu.CompilerParams(
            collective_id=0, has_side_effects=True, vmem_limit_bytes=40 * 1024 * 1024
        ),
    )(source_channel, spectra)
    return result.reshape(BLOCK, 8, 16)


def solution(mesh):
    return jax.shard_map(
        per_device,
        mesh=mesh,
        in_specs=(P("win", None, "rcv", None), P()),
        out_specs=P("win", None, "rcv"),
        check_vma=False,
    )
```

time: 75.6 us -> 48.1 us (0.64)
  Pallas kernels: 27.9 us -> 45.5 us
  waiting for transfers between devices: 14.2 us -> 0 us
  other arithmetic: 12.5 us -> 0 us
  starting transfers between devices: 10.3 us -> 0 us
  local copies, waits for them, and re-layouts: 6.31 us -> 2.39 us
  matrix products: 3.9 us -> 0 us
    pallas_call x1, Pallas kernels: 27.9 us -> 45.5 us  [per_device(): pl.pallas_call(kernel, out_shape=jax.ShapeDtypeStruct((BLOCK, PAIRS), f32...]
    all_to_all x1 -> x0, waiting for transfers between devices: 14.2 us -> none  [per_device(): lax.all_to_all(jnp.broadcast_to(own_part[None], (8, *own_part.shape)), 'r...]
    all_to_all x1 -> x0, starting transfers between devices: 10.3 us -> none  [per_device(): lax.all_to_all(jnp.broadcast_to(own_part[None], (8, *own_part.shape)), 'r...]
    convert_element_type x3 -> x0, other arithmetic: 8.35 us -> none  [the longest x1 6 us: make_basis(): (-sin).astype(jnp.bfloat16).reshape(L, bin_count)]
    dot_general x3 -> x0, matrix products: 3.9 us -> none  [the longest x1 1.33 us: per_device(): jnp.einsum('sr,wcrf->wcsf', onehot, spectra, preferred_element_type=jnp.f...]
    mul x1 -> x0, other arithmetic: 2.15 us -> none  [make_basis(): coarse_s * factor]
    sin x1 -> x0, other arithmetic: 1.73 us -> none  [tables(): return (jnp.cos(angle), jnp.sin(angle))]
    broadcast_in_dim x1 -> x0, local copies, waits for them, and re-layouts: 1.61 us -> none  [per_device(): jnp.broadcast_to(own_part[None], (8, *own_part.shape))]
  transfers between devices with their start and end apart: 1 -> 0, of which waited for: 1 -> 0; matrix products, arithmetic and copies ran while one was open for 16% -> 0% of each run, Pallas kernels for 0% -> 0%
where the time goes in v2:
time: 48.1 us; the launch traced here: 47.9 us
  Pallas kernels  45.5 us (95%)
  local copies, waits for them, and re-layouts  2.39 us (5%)
    pallas_call x1, Pallas kernels, per_device(): pl.pallas_call(kernel, out_shape=jax.ShapeDtypeStruct((BLOCK, PAIRS), f32...  45.5 us
    unnamed x4, local copies, waits for them, and re-layouts  1.7 us

profile of v2, /device:TPU:1, one launch (start us, length us, event | category | flops | bytes accessed | tf_op | source)
XLA Modules:
  0.0 47.9 jit_solution(15958698898691867029)
XLA Ops:
  0.0 0.0 copy-start
  0.0 1.0 %copy-done = bf16[2,2,16,4096]{3,2,1,0:T(8,128)(2,1)S(1)} copy-done((bf16[2,2,16,4096]{3,2,1,0:T(8,128)(2,1)S(1)}, bf16[2,2,16,4096]{3,2,1,0:T(8,128)(2,1)}, u32[]{:S(2)}) %copy-start) | copy-done | bytes 524312
  1.0 0.0 copy-start.1
  1.0 0.7 %copy-done.1 = s32[8]{0:T(128)S(1)} copy-done((s32[8]{0:T(128)S(1)}, s32[8]{0:T(128)}, u32[]{:S(2)}) %copy-start.1) | copy-done | bytes 56
  1.7 45.5 %shard_map.28 = f32[8,128]{1,0:T(8,128)S(1)} custom-call(s32[8]{0:T(128)S(1)} %copy-done.1, bf16[2,2,16,4096]{3,2,1,0:T(8,128)(2,1)S(1)} %copy-done), custom_call_target="tpu_custom_call" | custom-call | tf_op jit(solution)/shard_map/pallas_call | solution.py:256
  47.2 0.7 %reshape.3 = f32[8,8,16]{2,1,0:T(8,128)} reshape(f32[8,128]{1,0:T(8,128)S(1)} %shard_map.28) | data formatting | bytes 8192 | tf_op jit(solution)/shard_map/reshape | solution.py:288
Async XLA Ops:
  0.0 1.0 %copy-start = (bf16[2,2,16,4096]{3,2,1,0:T(8,128)(2,1)S(1)}, bf16[2,2,16,4096]{3,2,1,0:T(8,128)(2,1)}, u32[]{:S(2)}) copy-start(bf16[2,2,16,4096]{3,2,1,0:T(8,128)(2,1)} %spectra_ref.1) | copy-start | bytes 1572868
  1.0 0.7 %copy-start.1 = (s32[8]{0:T(128)S(1)}, s32[8]{0:T(128)}, u32[]{:S(2)}) copy-start(s32[8]{0:T(128)} %channel_ref.1) | copy-start | bytes 100

commit v3 on v2

--- a/solution.py
+++ b/solution.py
@@ -111,12 +111,15 @@
     pltpu.make_async_copy(ref, ref, sem).wait()
 
 
+ORDER = (0, 2, 1, 3)
+
+
 def kernel(
-    channel_ref, spectra_ref, o_ref,
-    spec, own, pair, summed, parts, sources, source_f,
+    channel_hbm, spectra_ref, o_ref,
+    channel_ref, spec, own, pair, first, got1, second, got2, sources, source_f,
     coarse_c, coarse_s, fine_c, fine_s, basis_c, basis_s, cross_r, cross_i, acc_c, acc_s,
     blocks, got, vals,
-    spec_sem, pair_s, pair_r, part_s, part_r, all_s, all_r, to_s, to_r, send_s, send_r,
+    chan_sem, spec_sem, pair_s, pair_r, one_s, one_r, two_s, two_r, to_s, to_r, send_s, send_r, near, mid, far,
 ):
     me = lax.axis_index("win")
     z, x = me // NX, lax.rem(me, NX)
@@ -125,102 +128,113 @@
     other = 1 - core
     peers = [lax.rem(z + dz, NZ) * NX + lax.rem(x + dx, NX) for dz, dx in offsets()]
     partner = {"rcv": 2 * y + other}
-    across = {d: {"rcv": 2 * lax.rem(y + d, NY) + core} for d in (1, 2, 3)}
-    quarter = {d: lax.rem(y + NY - d, NY) for d in range(NY)}
-
-    loads = [
-        pltpu.make_async_copy(spectra_ref.at[:, :, :, pl.ds(q * QUARTER, QUARTER)], spec.at[q], spec_sem.at[q])
-        for q in range(NY)
-    ]
-    for load in loads:
-        load.start()
+    left = {"rcv": 2 * (y + 1 - 2 * lax.rem(y, 2)) + core}
+    right = {"rcv": 2 * (NY - 1 - y) + core}
+
+    def along(dz):
+        return {"win": lax.rem(z + NZ + dz, NZ) * NX + x}
+
+    loads = {
+        q: pltpu.make_async_copy(spectra_ref.at[:, :, :, pl.ds(q * QUARTER, QUARTER)], spec.at[q], spec_sem.at[q])
+        for q in ORDER
+    }
+    for q in ORDER:
+        loads[q].start()
+    channels = pltpu.make_async_copy(channel_hbm, channel_ref, chan_sem)
+    channels.start()
     barrier = pltpu.get_barrier_semaphore()
+    greeted = 0
     for d in range(1, 8):
         pl.semaphore_signal(barrier, inc=1, device_id={"rcv": lax.rem(mine + d, 8)}, device_id_type=MESH)
-    for peer in peers:
-        pl.semaphore_signal(barrier, inc=1, device_id={"win": peer}, device_id_type=MESH)
+        greeted += 1
+    for dz in (-1, 0, 1):
+        for dx in range(NX):
+            if dz or dx:
+                where = {"win": lax.rem(z + NZ + dz, NZ) * NX + lax.rem(x + dx, NX)}
+                pl.semaphore_signal(barrier, inc=1, device_id=where, device_id_type=MESH)
+                greeted += 1
 
     fill_table(fine_c, fine_s, 16, 1, False)
-    for load in loads:
-        load.wait()
+    fill_table(coarse_c, coarse_s, 24, 16, True)
+    channels.wait()
     row = lax.broadcasted_iota(jnp.int32, (16, 16), 0)
     column = lax.broadcasted_iota(jnp.int32, (16, 16), 1) + mine * 16
     onehot = jnp.zeros((16, 16), jnp.float32)
     for s in range(8):
         onehot = jnp.where((row == s) & (column == channel_ref[s]), 1.0, onehot)
     onehot = onehot.astype(jnp.bfloat16)
+    for q in ORDER:
+        loads[q].wait()
     for w in range(2):
         for q in range(NY):
             picked = [
                 jnp.dot(onehot, spec[q, w, c], preferred_element_type=jnp.float32)[:8] for c in range(2)
             ]
             own[w, q] = jnp.concatenate(picked, axis=0).astype(jnp.bfloat16)
-    pl.semaphore_wait(barrier, 7 + WIN - 1)
-
-    swap = remote(own.at[other], pair, pair_s, pair_r, partner)
-    swap.start()
-    fill_table(coarse_c, coarse_s, 24, 16, True)
-    swap.wait_recv()
-    for q in range(NY):
-        summed[q] = own[core, q] + pair[q]
-    scatter = [
-        remote(summed.at[lax.rem(y + d, NY)], parts.at[d - 1], part_s, part_r, across[d]) for d in (2, 1, 3)
-    ]
-    for copy in scatter:
-        copy.start()
+    pl.semaphore_wait(barrier, greeted)
+
+    for dz in (-1, 1):
+        pl.semaphore_signal(near, inc=1, device_id=along(dz), device_id_type=MESH)
+
+    swap = {q: remote(own.at[other, q], pair.at[q], pair_s, pair_r.at[q], partner) for q in ORDER}
+    for q in ORDER:
+        swap[q].start()
+    one = {q: remote(first.at[q], got1.at[q], one_s, one_r.at[q], left if q < 2 else right) for q in ORDER}
+    two = {q: remote(second.at[q], got2.at[q], two_s, two_r.at[q], right if q < 2 else left) for q in ORDER}
+    hand = {q: remote(sources.at[core, q], sources.at[core, q], to_s, to_r.at[q], partner) for q in ORDER}
+    for q in ORDER:
+        swap[q].wait_recv()
+        first[q] = own[core, q] + pair[q]
+        one[q].start()
+    pl.semaphore_wait(near, 2)
+    for dz in (-2, 2):
+        pl.semaphore_signal(mid, inc=1, device_id=along(dz), device_id_type=MESH)
     fill_basis(0, ROWS // 16, coarse_c, coarse_s, fine_c, fine_s, basis_c, basis_s)
-    wait_bytes(parts, part_r)
-    sources[core, y] = summed[y] + parts[0] + parts[1] + parts[2]
-    held = sources.at[core, y]
-    gather = {d: remote(held, held, all_s, all_r.at[d - 1], across[d]) for d in (2, 1, 3)}
-    for d in (2, 1, 3):
-        gather[d].start()
-
-    def hand(d):
-        there = sources.at[core, quarter[d]]
-        copy = remote(there, there, to_s, to_r.at[d], partner)
-        copy.start()
-        return copy
-
-    def compute(d):
-        q = quarter[d]
-        hands[d].wait_recv()
-        for w in range(2):
-            source_f[w] = sources[w, q].astype(jnp.float32)
-        for w in range(2):
-            for part in range(QUARTER // COLS):
-                cols = pl.ds(part * COLS, COLS)
-                p = spec[q, w, 0, :, cols].astype(jnp.float32)
-                i = spec[q, w, 1, :, cols].astype(jnp.float32)
-                for s in range(8):
-                    a = source_f[w, pl.ds(s, 1), cols]
-                    b = source_f[w, pl.ds(8 + s, 1), cols]
-                    rows = pl.ds(w * PAIRS + s * 16, 16)
-                    cross_r[d, rows, cols] = (a * p + b * i).astype(jnp.bfloat16)
-                    cross_i[d, rows, cols] = (b * p - a * i).astype(jnp.bfloat16)
-        dims = (((1,), (1,)), ((), ()))
-        sum_c = lax.dot_general(basis_c[q], cross_r[d], dims, preferred_element_type=jnp.float32)
-        sum_s = lax.dot_general(basis_s[q], cross_i[d], dims, preferred_element_type=jnp.float32)
-        if d == 0:
+    for q in ORDER:
+        one[q].wait_recv()
+        second[q] = first[q] + got1[q]
+        two[q].start()
+    pl.semaphore_wait(mid, 2)
+    for dz in (-4, 4):
+        pl.semaphore_signal(far, inc=1, device_id=along(dz), device_id_type=MESH)
+
+    def cross(q, at):
+        w = other if at else core
+        source_f[at] = sources[w, q].astype(jnp.float32)
+        for part in range(QUARTER // COLS):
+            cols = pl.ds(part * COLS, COLS)
+            p = spec[q, w, 0, :, cols].astype(jnp.float32)
+            i = spec[q, w, 1, :, cols].astype(jnp.float32)
+            for s in range(8):
+                a = source_f[at, pl.ds(s, 1), cols]
+                b = source_f[at, pl.ds(8 + s, 1), cols]
+                rows = pl.ds(at * PAIRS + s * 16, 16)
+                cross_r[q, rows, cols] = (a * p + b * i).astype(jnp.bfloat16)
+                cross_i[q, rows, cols] = (b * p - a * i).astype(jnp.bfloat16)
+
+    for q in ORDER:
+        two[q].wait_recv()
+        sources[core, q] = second[q] + got2[q]
+        hand[q].start()
+        cross(q, 0)
+    dims = (((1,), (1,)), ((), ()))
+    for n, q in enumerate(ORDER):
+        hand[q].wait_recv()
+        cross(q, 1)
+        sum_c = lax.dot_general(basis_c[q], cross_r[q], dims, preferred_element_type=jnp.float32)
+        sum_s = lax.dot_general(basis_s[q], cross_i[q], dims, preferred_element_type=jnp.float32)
+        if n == 0:
             acc_c[...] = sum_c
             acc_s[...] = sum_s
         else:
             acc_c[...] += sum_c
             acc_s[...] += sum_s
 
-    hands = {0: hand(0)}
-    compute(0)
-    for d in (1, 3, 2):
-        gather[d].wait_recv()
-        hands[d] = hand(d)
-    for d in (1, 3, 2):
-        compute(d)
-
     window = (2 * me).astype(jnp.float32)
-    scales = [1.0 + (window + w) * (1.0 / 128.0) for w in range(2)]
+    scales = [1.0 + (window + at) * (1.0 / 128.0) for at in range(2)]
     for ahead in (True, False):
-        first = 0 if ahead else 1
-        c, s = acc_c[pl.ds(first, HALF), :], acc_s[pl.ds(first, HALF), :]
+        start = 0 if ahead else 1
+        c, s = acc_c[pl.ds(start, HALF), :], acc_s[pl.ds(start, HALF), :]
         lags = c + s if ahead else c - s
         halves = [(lags[:, w * PAIRS : (w + 1) * PAIRS] * scales[w]).reshape(32, BLOCK, PAIRS) for w in range(2)]
         both = jnp.concatenate(halves, axis=1).astype(jnp.bfloat16)
@@ -229,6 +243,7 @@
         else:
             for m in range(32):
                 blocks[31 - m] = both[m]
+    pl.semaphore_wait(far, 2)
     for peer in peers:
         remote(blocks.at[peer], got.at[me], send_s, send_r, {"win": peer}).start()
     got[me] = blocks[me]
@@ -244,26 +259,26 @@
         for k in range(BLOCK):
             o_ref[pl.ds(BLOCK - 1 - k, 1), :] = center[k : k + 1]
 
-    swap.wait_send()
-    wait_bytes(parts, part_s)
-    wait_bytes(parts, all_s)
+    wait_bytes(pair, pair_s)
+    wait_bytes(first, one_s)
+    wait_bytes(second, two_s)
     wait_bytes(sources.at[0], to_s)
     wait_bytes(blocks.at[pl.ds(0, WIN - 1)], send_s)
 
 
 def per_device(spectra, source_channel):
     bf, f32, dma = jnp.bfloat16, jnp.float32, pltpu.SemaphoreType.DMA
+    regular = pltpu.SemaphoreType.REGULAR
     result = pl.pallas_call(
         kernel,
         out_shape=jax.ShapeDtypeStruct((BLOCK, PAIRS), f32),
-        in_specs=[pl.BlockSpec(memory_space=pltpu.SMEM), pl.BlockSpec(memory_space=pl.ANY)],
+        in_specs=[pl.BlockSpec(memory_space=pltpu.HBM), pl.BlockSpec(memory_space=pltpu.HBM)],
         out_specs=pl.BlockSpec(memory_space=pltpu.VMEM),
         scratch_shapes=[
+            pltpu.SMEM((8,), jnp.int32),
             pltpu.VMEM((NY, 2, 2, 16, QUARTER), bf),
             pltpu.VMEM((2, NY, 16, QUARTER), bf),
-            pltpu.VMEM((NY, 16, QUARTER), bf),
-            pltpu.VMEM((NY, 16, QUARTER), bf),
-            pltpu.VMEM((NY - 1, 16, QUARTER), bf),
+            *[pltpu.VMEM((NY, 16, QUARTER), bf) for _ in range(5)],
             pltpu.VMEM((2, NY, 16, QUARTER), bf),
             pltpu.VMEM((2, 16, QUARTER), f32),
             pltpu.VMEM((24, F), f32),
@@ -279,12 +294,17 @@
             pltpu.VMEM((WIN, 2 * BLOCK, PAIRS), bf),
             pltpu.VMEM((WIN, 2 * BLOCK, PAIRS), bf),
             pltpu.VMEM((2 * WIN, BLOCK, PAIRS), f32),
-            dma((NY,)), dma, dma, dma, dma, dma, dma((NY - 1,)), dma, dma((NY,)), dma, dma,
+            dma, dma((NY,)),
+            dma, dma((NY,)), dma, dma((NY,)), dma, dma((NY,)), dma, dma((NY,)), dma, dma,
+            regular, regular, regular,
         ],
         compiler_params=pltpu.CompilerParams(
             collective_id=0, has_side_effects=True, vmem_limit_bytes=40 * 1024 * 1024
         ),
-    )(source_channel, spectra)
+    )(
+        pltpu.with_memory_space_constraint(source_channel, pltpu.HBM),
+        pltpu.with_memory_space_constraint(spectra, pltpu.HBM),
+    )
     return result.reshape(BLOCK, 8, 16)
 
 

time: 48.1 us -> 41.5 us (0.86)
  Pallas kernels: 45.5 us -> 40.7 us
  local copies, waits for them, and re-layouts: 2.39 us -> 0.69 us
    pallas_call x1, Pallas kernels: 45.5 us -> 40.7 us  [per_device(): pl.pallas_call(kernel, out_shape=jax.ShapeDtypeStruct((BLOCK, PAIRS), f32...]
    unnamed x4 -> x0, local copies, waits for them, and re-layouts: 1.7 us -> none
where the time goes in v3:
time: 41.5 us; the launch traced here: 41.4 us
  Pallas kernels  40.7 us (98%)
  local copies, waits for them, and re-layouts  0.69 us (2%)
    pallas_call x1, Pallas kernels, per_device(): pl.pallas_call(kernel, out_shape=jax.ShapeDtypeStruct((BLOCK, PAIRS), f32...  40.7 us

profile of v3, /device:TPU:1, one launch (start us, length us, event | category | flops | bytes accessed | tf_op | source)
XLA Modules:
  0.0 41.4 jit_solution(10663506492669213663)
XLA Ops:
  0.0 40.7 %shard_map.28 = f32[8,128]{1,0:T(8,128)S(1)} custom-call(s32[8]{0:T(128)} %channel_hbm.1, bf16[2,2,16,4096]{3,2,1,0:T(8,128)(2,1)} %spectra_ref.1), custom_call_target="tpu_custom_call" | custom-call | tf_op jit(solution)/shard_map/pallas_call | solution.py:272
  40.7 0.7 %reshape.3 = f32[8,8,16]{2,1,0:T(8,128)} reshape(f32[8,128]{1,0:T(8,128)S(1)} %shard_map.28) | data formatting | bytes 8192 | tf_op jit(solution)/shard_map/reshape | solution.py:308

commit v4 on v3

v4 whole, which is shorter than its diff:
```python
import jax
import jax.numpy as jnp
from jax import lax
from jax.experimental import pallas as pl
from jax.experimental.pallas import tpu as pltpu
from jax.sharding import PartitionSpec as P

L = 512
F = 4096
ITERS = 5
TUKEY = 4.685
EPSILON = 1e-06
MESH = pl.DeviceIdType.MESH
NZ, NX, NY = 16, 4, 4
WIN = NZ * NX
BLOCK = L // WIN
HALF = L // 2
ROWS = HALF + 16
PIECES = 4
PIECE = F // PIECES
ORDER = tuple(p for pair in zip(range(PIECES // 2), range(PIECES // 2, PIECES)) for p in pair)
COLS = 512
PAIRS = 128


def signed(step, count):
    return step if step <= count // 2 else step - count


def offsets():
    found = [(dz, dx) for dz in range(NZ) for dx in range(NX) if dz or dx]
    return sorted(found, key=lambda o: -(4 * abs(signed(o[0], NZ)) + abs(signed(o[1], NX))))


def cos_sin(phase):
    turn = (phase + 1024) >> 11
    x = (phase - (turn << 11)).astype(jnp.float32) * (2.0 * jnp.pi / (2 * F))
    y = x * x
    s = x * (1.0 + y * (-1.0 / 6 + y * (1.0 / 120 + y * (-1.0 / 5040 + y * (1.0 / 362880)))))
    c = 1.0 + y * (-0.5 + y * (1.0 / 24 + y * (-1.0 / 720 + y * (1.0 / 40320))))
    odd = (turn & 1) == 1
    cos = jnp.where(odd, s, c)
    sin = jnp.where(odd, c, s)
    cos = jnp.where(((turn + 1) & 2) == 2, -cos, cos)
    sin = jnp.where((turn & 2) == 2, -sin, sin)
    return cos, sin


def fill_table(cos_ref, sin_ref, rows, step, scaled):
    for part in range(F // COLS):
        cols = pl.ds(part * COLS, COLS)
        freq = part * COLS + lax.broadcasted_iota(jnp.int32, (rows, COLS), 1)
        row = lax.broadcasted_iota(jnp.int32, (rows, COLS), 0)
        cos, sin = cos_sin((row * freq * step) & (2 * F - 1))
        if scaled:
            factor = jnp.where(freq == 0, 1.0, 2.0) * (1.0 / (8 * F) ** 0.5)
            cos, sin = cos * factor, sin * factor
        cos_ref[:, cols] = cos
        sin_ref[:, cols] = sin


def fill_basis(first, last, coarse_c, coarse_s, fine_c, fine_s, basis_c, basis_s):
    for part in range(F // COLS):
        cols = pl.ds(part * COLS, COLS)
        piece, start = divmod(part * COLS, PIECE)
        fc, fs = fine_c[:, cols], fine_s[:, cols]

        def one(g, _, cols=cols, piece=piece, start=start, fc=fc, fs=fs):
            cc, cs = coarse_c[pl.ds(g, 1), cols], coarse_s[pl.ds(g, 1), cols]
            rows = pl.ds(pl.multiple_of(g * 16, 16), 16)
            basis_c[piece, rows, start : start + COLS] = (cc * fc - cs * fs).astype(jnp.bfloat16)
            basis_s[piece, rows, start : start + COLS] = (-(cs * fc) - cc * fs).astype(jnp.bfloat16)
            return 0

        lax.fori_loop(first, last, one, 0)


def read_half(got, vals, at):
    sums = [None] * 8
    for w in range(WIN):
        value = got[at, w].astype(jnp.float32) * (1.0 / (1.0 + (2 * w + at) / 128.0))
        vals[at * WIN + w] = value
        sums[w % 8] = value if sums[w % 8] is None else sums[w % 8] + value
    return sum(sums[1:], sums[0])


def stack(total, vals):
    windows = 2 * WIN
    mean = total * (1.0 / windows)
    sums = [jnp.zeros_like(mean)] * 8
    for w in range(windows):
        dev = vals[w] - mean
        sums[w % 8] = sums[w % 8] + dev * dev
    var = sum(sums[1:], sums[0]) * (1.0 / windows)
    center = mean
    for _ in range(ITERS):
        shift = mean - center
        inverse = 1.0 / (TUKEY * TUKEY * (var + shift * shift + EPSILON))
        weights = [jnp.zeros_like(mean)] * 8
        moved = [jnp.zeros_like(mean)] * 8
        for w in range(windows):
            dev = vals[w] - center
            root = jnp.maximum(1.0 - dev * dev * inverse, 0.0)
            weight = root * root
            weights[w % 8] = weights[w % 8] + weight
            moved[w % 8] = moved[w % 8] + weight * dev
        center = center + sum(moved[1:], moved[0]) / sum(weights[1:], weights[0])
    return center


def remote(src, dst, send_sem, recv_sem, where):
    return pltpu.make_async_remote_copy(src, dst, send_sem, recv_sem, device_id=where, device_id_type=MESH)


def wait_bytes(ref, sem):
    pltpu.make_async_copy(ref, ref, sem).wait()


def kernel(
    channel_hbm, spectra_ref, o_ref,
    channel_ref, spec, own, pair, first, got1, second, got2, sources, source_f,
    coarse_c, coarse_s, fine_c, fine_s, basis_c, basis_s, cross_r, cross_i, acc_c, acc_s,
    blocks, got, vals,
    chan_sem, spec_sem, pair_s, pair_r, one_s, one_r, two_s, two_r, to_s, to_r, send_s, send_r,
    know,
):
    me = lax.axis_index("win")
    z, x = me // NX, lax.rem(me, NX)
    mine = lax.axis_index("rcv")
    y, core = mine // 2, lax.rem(mine, 2)
    other = 1 - core

    def at_offset(dz, dx):
        return lax.rem(z + NZ + dz, NZ) * NX + lax.rem(x + NX + dx, NX)

    partner = {"rcv": 2 * y + other}
    left = {"rcv": 2 * (y + 1 - 2 * lax.rem(y, 2)) + core}
    right = {"rcv": 2 * (NY - 1 - y) + core}

    loads = {
        p: pltpu.make_async_copy(spectra_ref.at[:, :, :, pl.ds(p * PIECE, PIECE)], spec.at[p], spec_sem.at[p])
        for p in ORDER
    }
    for p in ORDER:
        loads[p].start()
    channels = pltpu.make_async_copy(channel_hbm, channel_ref, chan_sem)
    channels.start()
    barrier = pltpu.get_barrier_semaphore()
    steps = {0: ((0, -1), (0, 1)), 1: ((-1, 0), (1, 0)), 2: ((-2, 0), (2, 0)), 3: ((-4, 0), (4, 0)), 4: ((-1, 0), (1, 0))}
    for where in (partner, left, right):
        pl.semaphore_signal(barrier, inc=1, device_id=where, device_id_type=MESH)
    for offset in steps[0] + steps[1]:
        pl.semaphore_signal(barrier, inc=1, device_id={"win": at_offset(*offset)}, device_id_type=MESH)

    def tell(n):
        for offset in steps[n]:
            pl.semaphore_signal(know.at[n], inc=1, device_id={"win": at_offset(*offset)}, device_id_type=MESH)

    def learn(n):
        pl.semaphore_wait(know.at[n], 2)

    fill_table(fine_c, fine_s, 16, 1, False)
    fill_table(coarse_c, coarse_s, 24, 16, True)
    channels.wait()
    row = lax.broadcasted_iota(jnp.int32, (16, 16), 0)
    column = lax.broadcasted_iota(jnp.int32, (16, 16), 1) + mine * 16
    onehot = jnp.zeros((16, 16), jnp.float32)
    for s in range(8):
        onehot = jnp.where((row == s) & (column == channel_ref[s]), 1.0, onehot)
    onehot = onehot.astype(jnp.bfloat16)
    for p in ORDER:
        loads[p].wait()
    for w in range(2):
        for p in range(PIECES):
            picked = [
                jnp.dot(onehot, spec[p, w, c], preferred_element_type=jnp.float32)[:8] for c in range(2)
            ]
            own[w, p] = jnp.concatenate(picked, axis=0).astype(jnp.bfloat16)
    pl.semaphore_wait(barrier, 7)
    tell(0)

    half = PIECES // 2
    swap = {p: remote(own.at[other, p], pair.at[p], pair_s, pair_r.at[p], partner) for p in ORDER}
    one = {p: remote(first.at[p], got1.at[p], one_s, one_r.at[p], left if p < half else right) for p in ORDER}
    two = {p: remote(second.at[p], got2.at[p], two_s, two_r.at[p], right if p < half else left) for p in ORDER}
    hand = {p: remote(sources.at[core, p], sources.at[core, p], to_s, to_r.at[p], partner) for p in ORDER}
    for p in ORDER:
        swap[p].start()
    for p in ORDER:
        swap[p].wait_recv()
        first[p] = own[core, p] + pair[p]
        one[p].start()
    learn(0)
    tell(1)
    fill_basis(0, 8, coarse_c, coarse_s, fine_c, fine_s, basis_c, basis_s)
    learn(1)
    tell(2)
    fill_basis(8, ROWS // 16, coarse_c, coarse_s, fine_c, fine_s, basis_c, basis_s)
    for p in ORDER:
        one[p].wait_recv()
        second[p] = first[p] + got1[p]
        two[p].start()
    learn(2)
    tell(3)

    dims = (((1,), (1,)), ((), ()))

    def compute(n, p, at):
        w = other if at else core
        source_f[at] = sources[w, p].astype(jnp.float32)
        for part in range(PIECE // COLS):
            cols = pl.ds(part * COLS, COLS)
            re = spec[p, w, 0, :, cols].astype(jnp.float32)
            im = spec[p, w, 1, :, cols].astype(jnp.float32)
            for s in range(8):
                a = source_f[at, pl.ds(s, 1), cols]
                b = source_f[at, pl.ds(8 + s, 1), cols]
                rows = pl.ds(s * 16, 16)
                cross_r[at, p, rows, cols] = (a * re + b * im).astype(jnp.bfloat16)
                cross_i[at, p, rows, cols] = (b * re - a * im).astype(jnp.bfloat16)
        sum_c = lax.dot_general(basis_c[p], cross_r[at, p], dims, preferred_element_type=jnp.float32)
        sum_s = lax.dot_general(basis_s[p], cross_i[at, p], dims, preferred_element_type=jnp.float32)
        if n == 0:
            acc_c[at] = sum_c
            acc_s[at] = sum_s
        else:
            acc_c[at] += sum_c
            acc_s[at] += sum_s

    def send(at):
        scale = 1.0 + ((2 * me).astype(jnp.float32) + at) * (1.0 / 128.0)
        plus = acc_c[at, pl.ds(0, HALF), :] + acc_s[at, pl.ds(0, HALF), :]
        blocks[at, pl.ds(32, 32)] = (plus * scale).reshape(32, BLOCK, PAIRS).astype(jnp.bfloat16)
        minus = acc_c[at, pl.ds(1, HALF), :] - acc_s[at, pl.ds(1, HALF), :]
        minus = (minus * scale).reshape(32, BLOCK, PAIRS).astype(jnp.bfloat16)
        for m in range(32):
            blocks[at, 31 - m] = minus[m]
        if at == 0:
            learn(4)
        for dz, dx in offsets():
            peer = at_offset(dz, dx)
            remote(blocks.at[at, peer], got.at[at, me], send_s.at[at], send_r.at[at], {"win": peer}).start()
        got[at, me] = blocks[at, me]

    for n, p in enumerate(ORDER):
        two[p].wait_recv()
        sources[core, p] = second[p] + got2[p]
        hand[p].start()
        if n == PIECES - 1:
            learn(3)
            tell(4)
        compute(n, p, 0)
    send(0)
    for n, p in enumerate(ORDER):
        hand[p].wait_recv()
        compute(n, p, 1)
    send(1)
    most = pl.ds(0, WIN - 1)
    wait_bytes(got.at[0, most], send_r.at[0])
    total = read_half(got, vals, 0)
    wait_bytes(got.at[1, most], send_r.at[1])
    center = stack(total + read_half(got, vals, 1), vals)

    @pl.when(me >= 32)
    def _():
        o_ref[...] = center

    @pl.when(me < 32)
    def _():
        for k in range(BLOCK):
            o_ref[pl.ds(BLOCK - 1 - k, 1), :] = center[k : k + 1]

    wait_bytes(pair, pair_s)
    wait_bytes(first, one_s)
    wait_bytes(second, two_s)
    wait_bytes(sources.at[0], to_s)
    for at in range(2):
        wait_bytes(blocks.at[at, most], send_s.at[at])


def per_device(spectra, source_channel):
    bf, f32, dma = jnp.bfloat16, jnp.float32, pltpu.SemaphoreType.DMA
    result = pl.pallas_call(
        kernel,
        out_shape=jax.ShapeDtypeStruct((BLOCK, PAIRS), f32),
        in_specs=[pl.BlockSpec(memory_space=pltpu.HBM), pl.BlockSpec(memory_space=pltpu.HBM)],
        out_specs=pl.BlockSpec(memory_space=pltpu.VMEM),
        scratch_shapes=[
            pltpu.SMEM((8,), jnp.int32),
            pltpu.VMEM((PIECES, 2, 2, 16, PIECE), bf),
            pltpu.VMEM((2, PIECES, 16, PIECE), bf),
            *[pltpu.VMEM((PIECES, 16, PIECE), bf) for _ in range(5)],
            pltpu.VMEM((2, PIECES, 16, PIECE), bf),
            pltpu.VMEM((2, 16, PIECE), f32),
            pltpu.VMEM((24, F), f32),
            pltpu.VMEM((24, F), f32),
            pltpu.VMEM((16, F), f32),
            pltpu.VMEM((16, F), f32),
            pltpu.VMEM((PIECES, ROWS, PIECE), bf),
            pltpu.VMEM((PIECES, ROWS, PIECE), bf),
            pltpu.VMEM((2, PIECES, PAIRS, PIECE), bf),
            pltpu.VMEM((2, PIECES, PAIRS, PIECE), bf),
            pltpu.VMEM((2, ROWS, PAIRS), f32),
            pltpu.VMEM((2, ROWS, PAIRS), f32),
            pltpu.VMEM((2, WIN, BLOCK, PAIRS), bf),
            pltpu.VMEM((2, WIN, BLOCK, PAIRS), bf),
            pltpu.VMEM((2 * WIN, BLOCK, PAIRS), f32),
            dma, dma((PIECES,)),
            dma, dma((PIECES,)), dma, dma((PIECES,)), dma, dma((PIECES,)), dma, dma((PIECES,)),
            dma((2,)), dma((2,)),
            pltpu.SemaphoreType.REGULAR((5,)),
        ],
        compiler_params=pltpu.CompilerParams(
            collective_id=0, has_side_effects=True, vmem_limit_bytes=40 * 1024 * 1024
        ),
    )(
        pltpu.with_memory_space_constraint(source_channel, pltpu.HBM),
        pltpu.with_memory_space_constraint(spectra, pltpu.HBM),
    )
    return result.reshape(BLOCK, 8, 16)


def solution(mesh):
    return jax.shard_map(
        per_device,
        mesh=mesh,
        in_specs=(P("win", None, "rcv", None), P()),
        out_specs=P("win", None, "rcv"),
        check_vma=False,
    )
```

time: 41.5 us -> 39.4 us (0.949)
  Pallas kernels: 40.7 us -> 38.4 us
    pallas_call x1, Pallas kernels: 40.7 us -> 38.4 us  [per_device(): pl.pallas_call(kernel, out_shape=jax.ShapeDtypeStruct((BLOCK, PAIRS), f32...]
where the time goes in v4:
time: 39.4 us; the launch traced here: 39.1 us
  Pallas kernels  38.4 us (97%)
  local copies, waits for them, and re-layouts  0.69 us (2%)
    pallas_call x1, Pallas kernels, per_device(): pl.pallas_call(kernel, out_shape=jax.ShapeDtypeStruct((BLOCK, PAIRS), f32...  38.4 us

profile of v4, /device:TPU:1, one launch (start us, length us, event | category | flops | bytes accessed | tf_op | source)
XLA Modules:
  0.0 39.1 jit_solution(4508969614115847020)
XLA Ops:
  0.0 38.4 %shard_map.28 = f32[8,128]{1,0:T(8,128)S(1)} custom-call(s32[8]{0:T(128)} %channel_hbm.1, bf16[2,2,16,4096]{3,2,1,0:T(8,128)(2,1)} %spectra_ref.1), custom_call_target="tpu_custom_call" | custom-call | tf_op jit(solution)/shard_map/pallas_call | solution.py:283
  38.4 0.7 %reshape.3 = f32[8,8,16]{2,1,0:T(8,128)} reshape(f32[8,128]{1,0:T(8,128)S(1)} %shard_map.28) | data formatting | bytes 8192 | tf_op jit(solution)/shard_map/reshape | solution.py:320

commit v5 on v4

--- a/solution.py
+++ b/solution.py
@@ -18,9 +18,12 @@
 ROWS = HALF + 16
 PIECES = 4
 PIECE = F // PIECES
+
+
 ORDER = tuple(p for pair in zip(range(PIECES // 2), range(PIECES // 2, PIECES)) for p in pair)
 COLS = 512
 PAIRS = 128
+LAST = (NZ // 2, NX // 2)
 
 
 def signed(step, count):
@@ -75,36 +78,39 @@
         lax.fori_loop(first, last, one, 0)
 
 
-def read_half(got, vals, at):
-    sums = [None] * 8
+def fold(sums):
+    return (sums[0] + sums[1]) + (sums[2] + sums[3]) + ((sums[4] + sums[5]) + (sums[6] + sums[7]))
+
+
+def read_half(got, vals, at, origin):
+    sums, squares = [0.0] * 8, [0.0] * 8
     for w in range(WIN):
         value = got[at, w].astype(jnp.float32) * (1.0 / (1.0 + (2 * w + at) / 128.0))
+        if origin is None:
+            origin = value
+        value = value - origin
         vals[at * WIN + w] = value
-        sums[w % 8] = value if sums[w % 8] is None else sums[w % 8] + value
-    return sum(sums[1:], sums[0])
-
-
-def stack(total, vals):
+        sums[w % 8] += value
+        squares[w % 8] += value * value
+    return origin, fold(sums), fold(squares)
+
+
+def stack(total, squares, vals):
     windows = 2 * WIN
     mean = total * (1.0 / windows)
-    sums = [jnp.zeros_like(mean)] * 8
-    for w in range(windows):
-        dev = vals[w] - mean
-        sums[w % 8] = sums[w % 8] + dev * dev
-    var = sum(sums[1:], sums[0]) * (1.0 / windows)
+    var = jnp.maximum(squares * (1.0 / windows) - mean * mean, 0.0)
     center = mean
     for _ in range(ITERS):
         shift = mean - center
         inverse = 1.0 / (TUKEY * TUKEY * (var + shift * shift + EPSILON))
-        weights = [jnp.zeros_like(mean)] * 8
-        moved = [jnp.zeros_like(mean)] * 8
+        weights, moved = [0.0] * 8, [0.0] * 8
         for w in range(windows):
             dev = vals[w] - center
             root = jnp.maximum(1.0 - dev * dev * inverse, 0.0)
             weight = root * root
-            weights[w % 8] = weights[w % 8] + weight
-            moved[w % 8] = moved[w % 8] + weight * dev
-        center = center + sum(moved[1:], moved[0]) / sum(weights[1:], weights[0])
+            weights[w % 8] += weight
+            moved[w % 8] += weight * dev
+        center = center + fold(moved) / fold(weights)
     return center
 
 
@@ -195,13 +201,13 @@
     fill_basis(0, 8, coarse_c, coarse_s, fine_c, fine_s, basis_c, basis_s)
     learn(1)
     tell(2)
-    fill_basis(8, ROWS // 16, coarse_c, coarse_s, fine_c, fine_s, basis_c, basis_s)
     for p in ORDER:
         one[p].wait_recv()
         second[p] = first[p] + got1[p]
         two[p].start()
     learn(2)
     tell(3)
+    fill_basis(8, ROWS // 16, coarse_c, coarse_s, fine_c, fine_s, basis_c, basis_s)
 
     dims = (((1,), (1,)), ((), ()))
 
@@ -235,11 +241,15 @@
         minus = (minus * scale).reshape(32, BLOCK, PAIRS).astype(jnp.bfloat16)
         for m in range(32):
             blocks[at, 31 - m] = minus[m]
-        if at == 0:
+        if at:
             learn(4)
-        for dz, dx in offsets():
-            peer = at_offset(dz, dx)
-            remote(blocks.at[at, peer], got.at[at, me], send_s.at[at], send_r.at[at], {"win": peer}).start()
+        for half in range(at + 1):
+            for dz, dx in offsets():
+                if half != at and (dz, dx) != LAST or half == at == 0 and (dz, dx) == LAST:
+                    continue
+                peer = at_offset(dz, dx)
+                there = got.at[half, me]
+                remote(blocks.at[half, peer], there, send_s.at[half], send_r.at[half], {"win": peer}).start()
         got[at, me] = blocks[at, me]
 
     for n, p in enumerate(ORDER):
@@ -257,9 +267,10 @@
     send(1)
     most = pl.ds(0, WIN - 1)
     wait_bytes(got.at[0, most], send_r.at[0])
-    total = read_half(got, vals, 0)
+    origin, total0, squares0 = read_half(got, vals, 0, None)
     wait_bytes(got.at[1, most], send_r.at[1])
-    center = stack(total + read_half(got, vals, 1), vals)
+    _, total1, squares1 = read_half(got, vals, 1, origin)
+    center = origin + stack(total0 + total1, squares0 + squares1, vals)
 
     @pl.when(me >= 32)
     def _():

time: 39.4 us -> 38.7 us (0.982)
  the two profiles are of different devices: /device:TPU:1 before, /device:TPU:2 now
where the time goes in v5:
time: 38.7 us; the launch traced here: 38.6 us
  Pallas kernels  37.9 us (98%)
  local copies, waits for them, and re-layouts  0.69 us (2%)
    pallas_call x1, Pallas kernels, per_device(): pl.pallas_call(kernel, out_shape=jax.ShapeDtypeStruct((BLOCK, PAIRS), f32...  37.9 us

profile of v5, /device:TPU:2, one launch (start us, length us, event | category | flops | bytes accessed | tf_op | source)
XLA Modules:
  0.0 38.6 jit_solution(10964336107067848663)
XLA Ops:
  0.0 37.9 %shard_map.28 = f32[8,128]{1,0:T(8,128)S(1)} custom-call(s32[8]{0:T(128)} %channel_hbm.1, bf16[2,2,16,4096]{3,2,1,0:T(8,128)(2,1)} %spectra_ref.1), custom_call_target="tpu_custom_call" | custom-call | tf_op jit(solution)/shard_map/pallas_call | solution.py:294
  37.9 0.7 %reshape.3 = f32[8,8,16]{2,1,0:T(8,128)} reshape(f32[8,128]{1,0:T(8,128)S(1)} %shard_map.28) | data formatting | bytes 8192 | tf_op jit(solution)/shard_map/reshape | solution.py:331

commit v6 on v5

--- a/solution.py
+++ b/solution.py
@@ -176,25 +176,30 @@
     onehot = onehot.astype(jnp.bfloat16)
     for p in ORDER:
         loads[p].wait()
-    for w in range(2):
-        for p in range(PIECES):
+
+    def pick(at):
+        for p in ORDER:
             picked = [
-                jnp.dot(onehot, spec[p, w, c], preferred_element_type=jnp.float32)[:8] for c in range(2)
+                jnp.dot(onehot, spec[p, other if at else core, c], preferred_element_type=jnp.float32)[:8]
+                for c in range(2)
             ]
-            own[w, p] = jnp.concatenate(picked, axis=0).astype(jnp.bfloat16)
+            own[at, p] = jnp.concatenate(picked, axis=0).astype(jnp.bfloat16)
+
+    pick(1)
     pl.semaphore_wait(barrier, 7)
     tell(0)
 
     half = PIECES // 2
-    swap = {p: remote(own.at[other, p], pair.at[p], pair_s, pair_r.at[p], partner) for p in ORDER}
+    swap = {p: remote(own.at[1, p], pair.at[p], pair_s, pair_r.at[p], partner) for p in ORDER}
     one = {p: remote(first.at[p], got1.at[p], one_s, one_r.at[p], left if p < half else right) for p in ORDER}
     two = {p: remote(second.at[p], got2.at[p], two_s, two_r.at[p], right if p < half else left) for p in ORDER}
     hand = {p: remote(sources.at[core, p], sources.at[core, p], to_s, to_r.at[p], partner) for p in ORDER}
     for p in ORDER:
         swap[p].start()
+    pick(0)
     for p in ORDER:
         swap[p].wait_recv()
-        first[p] = own[core, p] + pair[p]
+        first[p] = own[0, p] + pair[p]
         one[p].start()
     learn(0)
     tell(1)

time: 38.7 us -> 38.7 us (level)
  the two profiles are of different devices: /device:TPU:2 before, /device:TPU:32 now
where the time goes in v6:
time: 38.7 us; the launch traced here: 38.6 us
  Pallas kernels  37.9 us (98%)
  local copies, waits for them, and re-layouts  0.69 us (2%)
    pallas_call x1, Pallas kernels, per_device(): pl.pallas_call(kernel, out_shape=jax.ShapeDtypeStruct((BLOCK, PAIRS), f32...  37.9 us

profile of v6, /device:TPU:32, one launch (start us, length us, event | category | flops | bytes accessed | tf_op | source)
XLA Modules:
  0.0 38.6 jit_solution(4892351907866624568)
XLA Ops:
  0.0 37.9 %shard_map.28 = f32[8,128]{1,0:T(8,128)S(1)} custom-call(s32[8]{0:T(128)} %channel_hbm.1, bf16[2,2,16,4096]{3,2,1,0:T(8,128)(2,1)} %spectra_ref.1), custom_call_target="tpu_custom_call" | custom-call | tf_op jit(solution)/shard_map/pallas_call | solution.py:299
  37.9 0.7 %reshape.3 = f32[8,8,16]{2,1,0:T(8,128)} reshape(f32[8,128]{1,0:T(8,128)S(1)} %shard_map.28) | data formatting | bytes 8192 | tf_op jit(solution)/shard_map/reshape | solution.py:336
